TPU v7x, 32 devices: a whole 2x2x4 slice. The times are simulated.
32 devices in a mesh: pipe: 4 (over y, core), expert: 2 (over x), dp: 4 (over z).
Axes of the slice: x: 2, y: 2, z: 4, core: 2. Of those that a mesh axis runs over, the one named last changes fastest.
Arguments:
- tokens: bfloat16 [4, 1024, 3072], P('pipe', ('expert', 'dp')), may hold values from -6 to 6
- grad_out: bfloat16 [4, 1024, 3072], P('pipe', ('expert', 'dp')), may hold values from -6 to 6
- routes: int32 [4, 1024, 2], P('pipe', ('expert', 'dp')), may hold values from 0 to 7, as said below
- route_weights: float32 [4, 1024, 2], P('pipe', ('expert', 'dp')), may hold values from 0.1 to 0.9
- gate_weight: bfloat16 [4, 3072, 32768], P('pipe', None, ('expert', 'dp')), may hold values from -0.109375 to 0.109375
- up_weight: bfloat16 [4, 3072, 32768], P('pipe', None, ('expert', 'dp')), may hold values from -0.109375 to 0.109375
- down_weight: bfloat16 [4, 32768, 3072], P('pipe', ('expert', 'dp')), may hold values from -0.046875 to 0.046875
Outputs:
- upstream: bfloat16 [4, 1024, 3072], P('pipe', ('expert', 'dp'))
Inputs may be any that keep to these rules, and one draw needn't show every extreme that they name: `routes`: each row names two different experts. In every section, for each window expert e < 2, the tokens of one device that name e number 1 to 8, exactly 8 on some device, and the tokens of the whole section name e exactly 36 times.
All inputs are finite; a program needn't handle non-finite values.
Results may differ from a plain program's by a relative error of at most 0.0013.
Values may be sent and summed in bfloat16 or wider, within the bound.
No kernel may reach another device: no remote copies, remote signals or barrier semaphores. Data moves between devices by JAX's collectives and lax.ppermute only.
A program may use at most 192 MiB of HBM per device.

v0:
```python
import jax
import jax.numpy as jnp
from jax import lax
from jax.sharding import PartitionSpec as P

EF = 2
CAP = 8


def from_behind(value, axis, steps):
    count = lax.axis_size(axis)
    first, last = (max(0, -steps), min(count, count - steps))
    return lax.ppermute(value, axis, [(source, source + steps) for source in range(first, last)])


def hidden_grads(rows_in, rows_grad, gate_slice, up_slice, down_slice):
    gate_pre = jnp.dot(rows_in, gate_slice, preferred_element_type=jnp.float32)
    up_pre = jnp.dot(rows_in, up_slice, preferred_element_type=jnp.float32)
    sigmoid_gate = jax.nn.sigmoid(gate_pre)
    contract = (((1,), (1,)), ((), ()))
    act_grad = lax.dot_general(rows_grad, down_slice, contract, preferred_element_type=jnp.float32)
    gate_grad = (act_grad * up_pre * sigmoid_gate * (1.0 + gate_pre * (1.0 - sigmoid_gate))).astype(
        jnp.bfloat16
    )
    up_grad = (act_grad * gate_pre * sigmoid_gate).astype(jnp.bfloat16)
    result = lax.dot_general(gate_grad, gate_slice, contract, preferred_element_type=jnp.float32)
    return result + lax.dot_general(up_grad, up_slice, contract, preferred_element_type=jnp.float32)


def shards(tokens, grad_out, routes, route_weights, gate_weight, up_weight, down_weight):
    expert_count = lax.axis_size("expert")
    data_count = lax.axis_size("dp")
    device_count = expert_count * data_count
    group_size = device_count // EF
    inputs = tokens[0]
    upstream_grad = grad_out[0]
    picks = routes[0]
    pick_weights = route_weights[0]
    width = inputs.shape[1]
    capacity = CAP
    slot_range = jnp.arange(capacity, dtype=jnp.int32)
    upstream_float = upstream_grad.astype(jnp.float32)
    sent_inputs = []
    sent_grads = []
    sent_counts = []
    chosen_sets = []
    slot_places = []
    for expert in range(EF):
        first_pick = picks[:, 0] == expert
        second_pick = picks[:, 1] == expert
        chosen = first_pick | second_pick
        weight = jnp.where(first_pick, pick_weights[:, 0], 0.0) + jnp.where(
            second_pick, pick_weights[:, 1], 0.0
        )
        slot_place = jnp.cumsum(chosen.astype(jnp.int32)) - 1
        slot_table = ((slot_place[None, :] == slot_range[:, None]) & chosen[None, :]).astype(
            jnp.bfloat16
        )
        scaled = (weight[:, None] * upstream_float).astype(jnp.bfloat16)
        sent_inputs.append(
            jnp.dot(slot_table, inputs, preferred_element_type=jnp.float32).astype(jnp.bfloat16)
        )
        sent_grads.append(
            jnp.dot(slot_table, scaled, preferred_element_type=jnp.float32).astype(jnp.bfloat16)
        )
        sent_counts.append(jnp.sum(chosen.astype(jnp.int32)))
        chosen_sets.append(chosen)
        slot_places.append(jnp.clip(slot_place, 0, capacity - 1))
    stack_inputs = jnp.stack(sent_inputs)
    stack_grads = jnp.stack(sent_grads)
    stack_counts = jnp.stack(sent_counts)
    bound_inputs = jnp.repeat(stack_inputs, group_size, axis=0)
    bound_grads = jnp.repeat(stack_grads, group_size, axis=0)
    bound_counts = jnp.repeat(stack_counts, group_size)[:, None]
    recv_inputs, recv_grads, recv_counts = (
        lax.all_to_all(bound_inputs, ("expert", "dp"), split_axis=0, concat_axis=0, tiled=True),
        lax.all_to_all(bound_grads, ("expert", "dp"), split_axis=0, concat_axis=0, tiled=True),
        lax.all_to_all(bound_counts, ("expert", "dp"), split_axis=0, concat_axis=0, tiled=True),
    )
    rows_in = recv_inputs.reshape(device_count * capacity, width)
    rows_grad = recv_grads.reshape(device_count * capacity, width)
    counts_in = recv_counts[:, 0]
    live_slots = (slot_range[None, :] < counts_in[:, None]).reshape(-1)
    gate_slice = gate_weight[0]
    up_slice = up_weight[0]
    down_slice = down_weight[0]
    partial_value = hidden_grads(rows_in, rows_grad, gate_slice, up_slice, down_slice) * live_slots[
        :, None
    ].astype(jnp.float32)
    partial_bf = partial_value.astype(jnp.bfloat16).reshape(device_count, capacity, width)
    returned = lax.all_to_all(partial_bf, ("expert", "dp"), split_axis=0, concat_axis=0, tiled=True)
    summed = returned.astype(jnp.float32).reshape(EF, group_size, capacity, width).sum(axis=1)
    branch = jnp.zeros_like(upstream_float)
    for expert in range(EF):
        picked_rows = summed[expert][slot_places[expert]]
        branch = branch + jnp.where(chosen_sets[expert][:, None], picked_rows, 0.0)
    grad_in = (upstream_float + branch).astype(jnp.bfloat16)[None]
    return from_behind(grad_in, "pipe", -1)


def solution(mesh):
    placed = (
        P("pipe", ("expert", "dp"), None),
        P("pipe", ("expert", "dp"), None),
        P("pipe", ("expert", "dp"), None),
        P("pipe", ("expert", "dp"), None),
        P("pipe", None, ("expert", "dp")),
        P("pipe", None, ("expert", "dp")),
        P("pipe", ("expert", "dp"), None),
    )
    return jax.shard_map(
        shards,
        mesh=mesh,
        in_specs=placed,
        out_specs=P("pipe", ("expert", "dp"), None),
        check_vma=False,
    )
```

profile of v0, /device:TPU:1, one launch (start us, length us, event | category | flops | bytes accessed | tf_op | source)
XLA Modules:
  0.0 130.9 jit_solution(7416122396753780305)
XLA Ops:
  0.0 0.0 copy-start
  0.0 0.0 copy-start.2
  0.0 0.9 copy.15
  0.9 0.2 or_reduce_fusion
  1.1 0.7 convert_reduce_fusion.1
  1.8 1.4 %pad_add_fusion = s32[2]{0:T(128)S(1)} fusion(s32[1]{0:T(128)} %bitcast.16, s32[1]{0:T(128)} %bitcast.15), kind=kLoop, calls=%fused_computation.89 | loop fusion | flops 2 | bytes 16 | tf_op jit(solution)/shard_map/stack | solution.py:71
  3.2 0.1 broadcast_in_dim.55
  3.3 0.7 all_to_all.20
  4.0 6.4 %all-to-all-start.2 = ((s32[8,1,1]{2,1,0:T(1,128)}), s32[8,1,1]{2,1,0:T(1,128)S(1)}, u32[]{:S(2)}, u32[]{:S(2)}) async-start(s32[8,1,1]{2,1,0:T(1,128)} %all_to_all.20), calls=%async_computation.2 | async-start | bytes 8192 | tf_op jit(solution)/shard_map/all_to_all | solution.py:78
  10.3 0.8 copy.16
  11.1 0.2 add_reduce_fusion.1
  11.3 0.2 reduce-window.9
  11.5 0.1 fusion.70
  11.6 0.2 reduce-window.6
  11.8 0.1 fusion.69
  11.9 1.4 %fusion.44 = bf16[1,8,3072]{2,1,0:T(8,128)(2,1)S(1)} fusion(bf16[1,128,3072]{2,1,0:T(8,128)(2,1)} %param.8, f32[128]{0:T(128)S(1)} %get-tuple-element.9, s32[128]{0:T(128)S(1)} %get-tuple-element.6, pred[128]{0:T(512)(128)(4,1)S(1)} %get-tuple-element.19), kind=kOutput, calls=%fused_computation.24 | convolution fusion | flops 7497728 | bytes 836736 | tf_op jit(solution)/shard_map/dot_general | solution.py:64
  13.3 0.0 copy-done.2
  13.4 0.3 fusion.45
  13.7 0.0 copy-done
  13.7 0.2 fusion.46
  13.9 1.7 %all-to-all-done.2 = s32[8,1,1]{2,1,0:T(1,128)S(1)} async-done(((s32[8,1,1]{2,1,0:T(1,128)}), s32[8,1,1]{2,1,0:T(1,128)S(1)}, u32[]{:S(2)}, u32[]{:S(2)}) %all-to-all-start.2) | async-done | bytes 64 | tf_op jit(solution)/shard_map/all_to_all | solution.py:78
  15.6 0.8 broadcast_in_dim.53
  16.3 3.8 %all-to-all-start = ((bf16[8,8,3072]{2,1,0:T(8,128)(2,1)}), bf16[8,8,3072]{2,1,0:T(8,128)(2,1)S(1)}, u32[]{:S(2)}, u32[]{:S(2)}) async-start(bf16[8,8,3072]{2,1,0:T(8,128)(2,1)} %bitcast.5), calls=%async_computation | async-start | bytes 786432 | tf_op jit(solution)/shard_map/all_to_all | solution.py:77
  20.1 0.2 fusion.47
  20.4 0.2 reduce.6
  20.6 0.1 fusion.77
  20.7 0.1 reshape.211
  20.8 8.8 %all-to-all-done = bf16[8,8,3072]{2,1,0:T(8,128)(2,1)S(1)} async-done(((bf16[8,8,3072]{2,1,0:T(8,128)(2,1)}), bf16[8,8,3072]{2,1,0:T(8,128)(2,1)S(1)}, u32[]{:S(2)}, u32[]{:S(2)}) %all-to-all-start) | async-done | bytes 393248 | tf_op jit(solution)/shard_map/all_to_all | solution.py:77
  29.6 0.8 broadcast_in_dim.54
  30.4 5.2 %all-to-all-start.1 = ((bf16[8,8,3072]{2,1,0:T(8,128)(2,1)}), bf16[8,8,3072]{2,1,0:T(8,128)(2,1)S(1)}, u32[]{:S(2)}, u32[]{:S(2)}) async-start(bf16[8,8,3072]{2,1,0:T(8,128)(2,1)} %bitcast.11), calls=%async_computation.1 | async-start | bytes 786432 | tf_op jit(solution)/shard_map/all_to_all | solution.py:76
  35.6 12.4 %fusion.8 = f32[64,4096]{1,0:T(8,128)S(1)} fusion(bf16[1,4096,3072]{2,1,0:T(8,128)(2,1)} %param.13, bf16[8,8,3072]{2,1,0:T(8,128)(2,1)S(1)} %all-to-all-done), kind=kOutput, calls=%fused_computation.10 | convolution fusion | flops 1610612736 | bytes 26607616 | tf_op jit(solution)/shard_map/dot_general | solution.py:21
  48.0 0.0 all-to-all-done.1
  48.1 10.5 %fusion.2 = f32[64,4096]{1,0:T(8,128)S(1)} fusion(bf16[1,3072,4096]{2,1,0:T(8,128)(2,1)} %param.11, bf16[8,8,3072]{2,1,0:T(8,128)(2,1)S(1)} %all-to-all-done.1), kind=kOutput, calls=%fused_computation.4 | convolution fusion | flops 1610612736 | bytes 26607616 | tf_op jit(solution)/shard_map/dot_general | solution.py:17
  58.5 13.3 %fusion.4 = f32[64,3072]{1,0:T(8,128)} fusion(bf16[1,3072,4096]{2,1,0:T(8,128)(2,1)} %param.12, f32[64,4096]{1,0:T(8,128)S(1)} %fusion.8, f32[64,4096]{1,0:T(8,128)S(1)} %fusion.2), kind=kOutput, calls=%fused_computation.6 | convolution fusion | flops 1612185600 | bytes 28049408 | tf_op jit(solution)/shard_map/dot_general | solution.py:27
  71.8 20.9 %fusion.39 = bf16[8,8,3072]{2,1,0:T(8,128)(2,1)} fusion(f32[64,3072]{1,0:T(8,128)} %fusion.4, bf16[1,3072,4096]{2,1,0:T(8,128)(2,1)} %param.11, f32[64,4096]{1,0:T(8,128)S(1)} %fusion.8, bf16[1,3072,4096]{2,1,0:T(8,128)(2,1)} %param.12, f32[64,4096]{1,0:T(8,128)S(1)} %fusion.2, bf16[8,8,3072]{2,1,0:T(8,128)(2,1)S(1)} %all-to-all-done.1, f32[64]{0:T(128)S(1)} %reshape.211), kind=kOutput, calls=%fused_computation.19 | convolution fusion | flops 3224436736 | bytes 54001920 | tf_op jit(solution)/shard_map/dot_general | solution.py:26
  92.8 5.4 %all-to-all-start.3 = ((bf16[8,8,3072]{2,1,0:T(8,128)(2,1)}), bf16[8,8,3072]{2,1,0:T(8,128)(2,1)S(1)}, u32[]{:S(2)}, u32[]{:S(2)}) async-start(bf16[8,8,3072]{2,1,0:T(8,128)(2,1)} %fusion.39), calls=%async_computation.3 | async-start | bytes 786432 | tf_op jit(solution)/shard_map/all_to_all | solution.py:91
  98.2 8.7 %all-to-all-done.3 = bf16[8,8,3072]{2,1,0:T(8,128)(2,1)S(1)} async-done(((bf16[8,8,3072]{2,1,0:T(8,128)(2,1)}), bf16[8,8,3072]{2,1,0:T(8,128)(2,1)S(1)}, u32[]{:S(2)}, u32[]{:S(2)}) %all-to-all-start.3) | async-done | bytes 393248 | tf_op jit(solution)/shard_map/all_to_all | solution.py:91
  107.0 1.2 gather_fusion
  108.2 0.0 copy-start.3
  108.2 2.3 %gather_fusion.1 = f32[128,3072]{1,0:T(8,128)} fusion(f32[8,3072]{1,0:T(8,128)S(1)} %get-tuple-element.18, s32[1024]{0:T(1024)S(1)} %pad_clamp_fusion), kind=kCustom, calls=%fused_computation.1 | custom fusion | bytes 3146240 | tf_op jit(solution)/shard_map/gather | solution.py:95
  110.5 0.0 copy-done.3
  110.5 0.0 copy-start.1
  110.5 1.9 %fusion.52 = bf16[1,128,3072]{2,1,0:T(8,128)(2,1)S(1)} fusion(bf16[1,128,3072]{2,1,0:T(8,128)(2,1)S(1)} %copy-done.3, f32[128,3072]{1,0:T(8,128)} %gather_fusion.1, f32[128,3072]{1,0:T(8,128)S(1)} %gather_fusion, pred[128]{0:T(512)(128)(4,1)S(1)} %get-tuple-element.14, pred[128]{0:T(512)(128)(4,1)S(1)} %get-tuple-element.19), kind=kLoop, calls=%fused_computation.34 | loop fusion | flops 2359296 | bytes 4718848 | tf_op jit(solution)/shard_map/convert_element_type | solution.py:97
  112.4 6.8 %collective-permute-start = (bf16[1,128,3072]{2,1,0:T(8,128)(2,1)S(1)}, bf16[1,128,3072]{2,1,0:T(8,128)(2,1)S(1)}, u32[]{:S(2)}, u32[]{:S(2)}) collective-permute-start(bf16[1,128,3072]{2,1,0:T(8,128)(2,1)S(1)} %fusion.52), channel_id=1, source_target_pairs={{8,0},{16,8},{24,16},{9,1},{17,9},{25,17},{10,2},{18,10},{26,18},{... | collective-permute-start | bytes 2359304 | tf_op jit(solution)/shard_map/ppermute | solution.py:13
  119.2 10.8 %collective-permute-done = bf16[1,128,3072]{2,1,0:T(8,128)(2,1)S(1)} collective-permute-done((bf16[1,128,3072]{2,1,0:T(8,128)(2,1)S(1)}, bf16[1,128,3072]{2,1,0:T(8,128)(2,1)S(1)}, u32[]{:S(2)}, u32[]{:S(2)}) %collective-permute-start) | collective-permute-done | bytes 786464 | tf_op jit(solution)/shard_map/ppermute | solution.py:13
  130.0 0.9 copy.19
  130.9 0.0 copy-done.1
  (7 shorter events, 0.1 us)
Async XLA Ops:
  0.0 13.7 %copy-start = (bf16[1,128,3072]{2,1,0:T(8,128)(2,1)S(1)}, bf16[1,128,3072]{2,1,0:T(8,128)(2,1)}, u32[]{:S(2)}) copy-start(bf16[1,128,3072]{2,1,0:T(8,128)(2,1)} %param.7) | copy-start | bytes 2359300
  0.0 13.3 %copy-start.2 = (bf16[1,128,3072]{2,1,0:T(8,128)(2,1)S(1)}, bf16[1,128,3072]{2,1,0:T(8,128)(2,1)}, u32[]{:S(2)}) copy-start(bf16[1,128,3072]{2,1,0:T(8,128)(2,1)} %param.8) | copy-start | bytes 2359300
  4.0 11.6 %all-to-all-start.2 = ((s32[8,1,1]{2,1,0:T(1,128)}), s32[8,1,1]{2,1,0:T(1,128)S(1)}, u32[]{:S(2)}, u32[]{:S(2)}) async-start(s32[8,1,1]{2,1,0:T(1,128)} %all_to_all.20), calls=%async_computation.2 | async-start | bytes 8192 | tf_op jit(solution)/shard_map/all_to_all | solution.py:78
  16.3 13.3 %all-to-all-start = ((bf16[8,8,3072]{2,1,0:T(8,128)(2,1)}), bf16[8,8,3072]{2,1,0:T(8,128)(2,1)S(1)}, u32[]{:S(2)}, u32[]{:S(2)}) async-start(bf16[8,8,3072]{2,1,0:T(8,128)(2,1)} %bitcast.5), calls=%async_computation | async-start | bytes 786432 | tf_op jit(solution)/shard_map/all_to_all | solution.py:77
  30.4 17.7 %all-to-all-start.1 = ((bf16[8,8,3072]{2,1,0:T(8,128)(2,1)}), bf16[8,8,3072]{2,1,0:T(8,128)(2,1)S(1)}, u32[]{:S(2)}, u32[]{:S(2)}) async-start(bf16[8,8,3072]{2,1,0:T(8,128)(2,1)} %bitcast.11), calls=%async_computation.1 | async-start | bytes 786432 | tf_op jit(solution)/shard_map/all_to_all | solution.py:76
  92.8 14.2 %all-to-all-start.3 = ((bf16[8,8,3072]{2,1,0:T(8,128)(2,1)}), bf16[8,8,3072]{2,1,0:T(8,128)(2,1)S(1)}, u32[]{:S(2)}, u32[]{:S(2)}) async-start(bf16[8,8,3072]{2,1,0:T(8,128)(2,1)} %fusion.39), calls=%async_computation.3 | async-start | bytes 786432 | tf_op jit(solution)/shard_map/all_to_all | solution.py:91
  108.2 2.3 %copy-start.3 = (bf16[1,128,3072]{2,1,0:T(8,128)(2,1)S(1)}, bf16[1,128,3072]{2,1,0:T(8,128)(2,1)}, u32[]{:S(2)}) copy-start(bf16[1,128,3072]{2,1,0:T(8,128)(2,1)} %param.8) | copy-start | bytes 2359300
  110.5 20.4 %copy-start.1 = (bf16[1,128,3072]{2,1,0:T(8,128)(2,1)S(1)}, bf16[1,128,3072]{2,1,0:T(8,128)(2,1)}, u32[]{:S(2)}) copy-start(bf16[1,128,3072]{2,1,0:T(8,128)(2,1)} %param.7) | copy-start | bytes 2359300
  112.4 17.6 %collective-permute-start = (bf16[1,128,3072]{2,1,0:T(8,128)(2,1)S(1)}, bf16[1,128,3072]{2,1,0:T(8,128)(2,1)S(1)}, u32[]{:S(2)}, u32[]{:S(2)}) collective-permute-start(bf16[1,128,3072]{2,1,0:T(8,128)(2,1)S(1)} %fusion.52), channel_id=1, source_target_pairs={{8,0},{16,8},{24,16},{9,1},{17,9},{25,17},{10,2},{18,10},{26,18},{... | collective-permute-start | bytes 2359304 | tf_op jit(solution)/shard_map/ppermute | solution.py:13
where the time goes:
time: 131 us
  matrix products  59.3 us (45%)
  waiting for transfers between devices  30 us (23%)
  starting transfers between devices  27.5 us (21%)
  local copies, waits for them, and re-layouts  8.41 us (6%)
  other arithmetic  5.42 us (4%)
    dot_general x1, matrix products, hidden_grads(): lax.dot_general(gate_grad, gate_slice, contract, preferred_element_type=j...  20.9 us
    dot_general x1, matrix products, hidden_grads(): lax.dot_general(up_grad, up_slice, contract, preferred_element_type=jnp.f...  13.3 us
    dot_general x1, matrix products, hidden_grads(): lax.dot_general(rows_grad, down_slice, contract, preferred_element_type=j...  12.4 us
    ppermute x1, waiting for transfers between devices, from_behind(): lax.ppermute(value, axis, [(source, source + steps) for source in range(f...  10.8 us
    dot_general x1, matrix products, hidden_grads(): gate_pre = jnp.dot(rows_in, gate_slice, preferred_element_type=jnp.float32)  10.5 us
    all_to_all x1, waiting for transfers between devices, shards(): lax.all_to_all(bound_grads, ('expert', 'dp'), split_axis=0, concat_axis=0...  8.85 us
    all_to_all x1, waiting for transfers between devices, shards(): lax.all_to_all(partial_bf, ('expert', 'dp'), split_axis=0, concat_axis=0,...  8.71 us
    ppermute x1, starting transfers between devices, from_behind(): lax.ppermute(value, axis, [(source, source + steps) for source in range(f...  6.76 us
  transfers between devices with their start and end apart: 5, of which 4 were waited for; matrix products, arithmetic and copies ran while one was open for 13% of the time, Pallas kernels for 0%

commit v1 on v0

--- a/solution.py
+++ b/solution.py
@@ -5,6 +5,30 @@
 
 EF = 2
 CAP = 8
+
+
+def split_up(x, dim, count):
+    shape = x.shape
+    pieces = x.reshape(*shape[:dim], count, shape[dim] // count, *shape[dim + 1 :])
+    return jnp.moveaxis(pieces, dim, 0)
+
+
+def laid_out(pieces, dim):
+    pieces = jnp.moveaxis(pieces, 0, dim)
+    shape = pieces.shape
+    return pieces.reshape(*shape[:dim], shape[dim] * shape[dim + 1], *shape[dim + 2 :])
+
+
+def exchange_directly(x, axis, split_dim, concat_dim):
+    size, position = (lax.axis_size(axis), lax.axis_index(axis))
+    pieces = split_up(x, split_dim, size)
+    filled = pieces
+    for step in range(1, size):
+        target, source = ((position + step) % size, (position - step) % size)
+        sent = lax.dynamic_index_in_dim(pieces, target, 0)
+        theirs = lax.ppermute(sent, axis, [(i, (i + step) % size) for i in range(size)])
+        filled = lax.dynamic_update_slice_in_dim(filled, theirs, source, axis=0)
+    return laid_out(filled, concat_dim)
 
 
 def from_behind(value, axis, steps):
@@ -73,7 +97,7 @@
     bound_grads = jnp.repeat(stack_grads, group_size, axis=0)
     bound_counts = jnp.repeat(stack_counts, group_size)[:, None]
     recv_inputs, recv_grads, recv_counts = (
-        lax.all_to_all(bound_inputs, ("expert", "dp"), split_axis=0, concat_axis=0, tiled=True),
+        exchange_directly(bound_inputs, ("expert", "dp"), 0, 0),
         lax.all_to_all(bound_grads, ("expert", "dp"), split_axis=0, concat_axis=0, tiled=True),
         lax.all_to_all(bound_counts, ("expert", "dp"), split_axis=0, concat_axis=0, tiled=True),
     )

time: 131 us -> 134 us (1.023)
  starting transfers between devices: 27.5 us -> 35.8 us
  waiting for transfers between devices: 30 us -> 26.6 us
  local copies, waits for them, and re-layouts: 8.41 us -> 7.06 us
    ppermute x0 -> x7, starting transfers between devices: none -> 13.7 us  [exchange_directly(): lax.ppermute(sent, axis, [(i, (i + step) % size) for i in range(size)])]
    all_to_all x1, waiting for transfers between devices: 8.85 us -> 0.01 us  [shards(): lax.all_to_all(bound_grads, ('expert', 'dp'), split_axis=0, concat_axis=0...]
    ppermute x0 -> x7, waiting for transfers between devices: none -> 5.75 us  [exchange_directly(): lax.ppermute(sent, axis, [(i, (i + step) % size) for i in range(size)])]
    all_to_all x1 -> x0, starting transfers between devices: 5.21 us -> none  [shards(): lax.all_to_all(bound_inputs, ('expert', 'dp'), split_axis=0, concat_axis=...]
  transfers between devices with their start and end apart: 5 -> 11, of which waited for: 4 -> 5; matrix products, arithmetic and copies ran while one was open for 13% -> 10% of each run, Pallas kernels for 0% -> 0%
where the time goes in v1:
time: 134 us
  matrix products  58.2 us (43%)
  starting transfers between devices  35.8 us (27%)
  waiting for transfers between devices  26.6 us (20%)
  local copies, waits for them, and re-layouts  7.06 us (5%)
  other arithmetic  5.4 us (4%)
    dot_general x1, matrix products, hidden_grads(): lax.dot_general(gate_grad, gate_slice, contract, preferred_element_type=j...  20.9 us
    ppermute x7, starting transfers between devices, exchange_directly(): lax.ppermute(sent, axis, [(i, (i + step) % size) for i in range(size)])  13.7 us
    dot_general x1, matrix products, hidden_grads(): lax.dot_general(up_grad, up_slice, contract, preferred_element_type=jnp.f...  13.3 us
    dot_general x1, matrix products, hidden_grads(): lax.dot_general(rows_grad, down_slice, contract, preferred_element_type=j...  12.4 us
    ppermute x1, waiting for transfers between devices, from_behind(): lax.ppermute(value, axis, [(source, source + steps) for source in range(f...  10.8 us
    dot_general x1, matrix products, hidden_grads(): gate_pre = jnp.dot(rows_in, gate_slice, preferred_element_type=jnp.float32)  10.5 us
    all_to_all x1, waiting for transfers between devices, shards(): lax.all_to_all(partial_bf, ('expert', 'dp'), split_axis=0, concat_axis=0,...  8.68 us
    ppermute x1, starting transfers between devices, from_behind(): lax.ppermute(value, axis, [(source, source + steps) for source in range(f...  6.99 us
  transfers between devices with their start and end apart: 11, of which 5 were waited for; matrix products, arithmetic and copies ran while one was open for 10% of the time, Pallas kernels for 0%

profile of v1, /device:TPU:1, one launch (start us, length us, event | category | flops | bytes accessed | tf_op | source)
XLA Modules:
  0.0 133.6 jit_solution(15699210228304034011)
XLA Ops:
  0.0 0.9 copy.15
  0.9 0.2 or_reduce_fusion
  1.0 0.0 copy-start.4
  1.1 0.7 convert_reduce_fusion.1
  1.8 1.4 %pad_add_fusion = s32[2]{0:T(128)S(1)} fusion(s32[1]{0:T(128)} %bitcast.16, s32[1]{0:T(128)} %bitcast.15), kind=kLoop, calls=%fused_computation.103 | loop fusion | flops 2 | bytes 16 | tf_op jit(solution)/shard_map/stack | solution.py:95
  3.2 0.1 broadcast_in_dim.55
  3.3 0.7 all_to_all.16
  3.9 6.4 %all-to-all-start.1 = ((s32[8,1,1]{2,1,0:T(1,128)}), s32[8,1,1]{2,1,0:T(1,128)S(1)}, u32[]{:S(2)}, u32[]{:S(2)}) async-start(s32[8,1,1]{2,1,0:T(1,128)} %all_to_all.16), calls=%async_computation.1 | async-start | bytes 8192 | tf_op jit(solution)/shard_map/all_to_all | solution.py:102
  10.3 0.0 copy-start.2
  10.3 0.2 reduce-window.9
  10.5 0.1 fusion.70
  10.6 0.2 reduce-window.6
  10.8 0.1 fusion.69
  10.9 0.2 fusion.46
  11.1 0.2 fusion.47
  11.4 1.5 %collective-permute-start = (bf16[1,1,8,3072]{3,2,0,1:T(8,128)(2,1)S(1)}, bf16[1,1,8,3072]{3,2,0,1:T(8,128)(2,1)S(1)}, u32[]{:S(2)}, u32[]{:S(2)}) collective-permute-start(bf16[1,1,8,3072]{3,2,0,1:T(8,128)(2,1)S(1)} %constant_dynamic-slice_fusion.6), channel_id=1, source_target_pairs={{0,1},{1,2},{2,3},{3,4},{4,5},{5,6},{6,7},{7,0},{8,9},{9,10},{10,1... | collective-permute-start | bytes 147464 | tf_op jit(solution)/shard_map/ppermute | solution.py:29
  12.9 0.1 copy.16
  13.0 0.2 add_reduce_fusion.1
  13.2 0.3 fusion.44
  13.5 0.3 fusion.45
  14.1 1.4 %all-to-all-done.1 = s32[8,1,1]{2,1,0:T(1,128)S(1)} async-done(((s32[8,1,1]{2,1,0:T(1,128)}), s32[8,1,1]{2,1,0:T(1,128)S(1)}, u32[]{:S(2)}, u32[]{:S(2)}) %all-to-all-start.1) | async-done | bytes 64 | tf_op jit(solution)/shard_map/all_to_all | solution.py:102
  15.5 0.8 broadcast_in_dim.53
  16.3 3.5 %all-to-all-start = ((bf16[8,8,3072]{2,1,0:T(8,128)(2,1)}), bf16[8,8,3072]{2,1,0:T(8,128)(2,1)S(1)}, u32[]{:S(2)}, u32[]{:S(2)}) async-start(bf16[8,8,3072]{2,1,0:T(8,128)(2,1)} %bitcast.5), calls=%async_computation | async-start | bytes 786432 | tf_op jit(solution)/shard_map/all_to_all | solution.py:101
  19.8 0.2 reduce.6
  20.0 0.0 collective-permute-done
  20.1 2.3 %collective-permute-start.1 = (bf16[1,1,8,3072]{3,2,0,1:T(8,128)(2,1)S(1)}, bf16[1,1,8,3072]{3,2,0,1:T(8,128)(2,1)S(1)}, u32[]{:S(2)}, u32[]{:S(2)}) collective-permute-start(bf16[1,1,8,3072]{3,2,0,1:T(8,128)(2,1)S(1)} %get-tuple-element.22), channel_id=1, source_target_pairs={{0,2},{1,3},{2,4},{3,5},{4,6},{5,7},{6,0},{7,1},{8,10},{9,11},{10,... | collective-permute-start | bytes 147464 | tf_op jit(solution)/shard_map/ppermute | solution.py:29
  22.4 0.1 fusion.77
  22.4 0.1 reshape.203
  22.5 2.1 %collective-permute-start.6 = (bf16[1,1,8,3072]{3,2,0,1:T(8,128)(2,1)S(1)}, bf16[1,1,8,3072]{3,2,0,1:T(8,128)(2,1)S(1)}, u32[]{:S(2)}, u32[]{:S(2)}) collective-permute-start(bf16[1,1,8,3072]{3,2,0,1:T(8,128)(2,1)S(1)} %get-tuple-element.17), channel_id=1, source_target_pairs={{0,7},{1,0},{2,1},{3,2},{4,3},{5,4},{6,5},{7,6},{8,15},{9,8},{10,9... | collective-permute-start | bytes 147464 | tf_op jit(solution)/shard_map/ppermute | solution.py:29
  24.6 1.2 collective-permute-start.5
  25.8 0.3 collective-permute-start.4
  26.1 0.1 collective-permute-start.3
  26.2 3.8 %collective-permute-done.1 = bf16[1,1,8,3072]{3,2,0,1:T(8,128)(2,1)S(1)} collective-permute-done((bf16[1,1,8,3072]{3,2,0,1:T(8,128)(2,1)S(1)}, bf16[1,1,8,3072]{3,2,0,1:T(8,128)(2,1)S(1)}, u32[]{:S(2)}, u32[]{:S(2)}) %collective-permute-start.1) | collective-permute-done | bytes 49184 | tf_op jit(solution)/shard_map/ppermute | solution.py:29
  30.0 6.2 %collective-permute-start.2 = (bf16[1,1,8,3072]{3,2,0,1:T(8,128)(2,1)S(1)}, bf16[1,1,8,3072]{3,2,0,1:T(8,128)(2,1)S(1)}, u32[]{:S(2)}, u32[]{:S(2)}) collective-permute-start(bf16[1,1,8,3072]{3,2,0,1:T(8,128)(2,1)S(1)} %get-tuple-element.21), channel_id=1, source_target_pairs={{0,3},{1,4},{2,5},{3,6},{4,7},{5,0},{6,1},{7,2},{8,11},{9,12},{10,... | collective-permute-start | bytes 147464 | tf_op jit(solution)/shard_map/ppermute | solution.py:29
  36.2 1.9 %collective-permute-done.2 = bf16[1,1,8,3072]{3,2,0,1:T(8,128)(2,1)S(1)} collective-permute-done((bf16[1,1,8,3072]{3,2,0,1:T(8,128)(2,1)S(1)}, bf16[1,1,8,3072]{3,2,0,1:T(8,128)(2,1)S(1)}, u32[]{:S(2)}, u32[]{:S(2)}) %collective-permute-start.2) | collective-permute-done | bytes 49184 | tf_op jit(solution)/shard_map/ppermute | solution.py:29
  38.3 10.5 %fusion.2 = f32[64,4096]{1,0:T(8,128)S(1)} fusion(bf16[1,3072,4096]{2,1,0:T(8,128)(2,1)} %param.11, bf16[8,1,8,3072]{3,2,0,1:T(8,128)(2,1)S(1)} %constant_dynamic-update-slice_fusion), kind=kOutput, calls=%fused_computation.4 | convolution fusion | flops 1610612736 | bytes 26607616 | tf_op jit(solution)/shard_map/dot_general | solution.py:41
  48.8 12.4 %fusion.8 = f32[64,4096]{1,0:T(8,128)S(1)} fusion(bf16[1,4096,3072]{2,1,0:T(8,128)(2,1)} %param.13, bf16[8,8,3072]{2,1,0:T(8,128)(2,1)S(1)} %all-to-all-done), kind=kOutput, calls=%fused_computation.10 | convolution fusion | flops 1610612736 | bytes 26607616 | tf_op jit(solution)/shard_map/dot_general | solution.py:45
  61.2 13.3 %fusion.4 = f32[64,3072]{1,0:T(8,128)} fusion(bf16[1,3072,4096]{2,1,0:T(8,128)(2,1)} %param.12, f32[64,4096]{1,0:T(8,128)S(1)} %fusion.8, f32[64,4096]{1,0:T(8,128)S(1)} %fusion.2), kind=kOutput, calls=%fused_computation.6 | convolution fusion | flops 1612185600 | bytes 28049408 | tf_op jit(solution)/shard_map/dot_general | solution.py:51
  74.5 20.9 %fusion.39 = bf16[8,8,3072]{2,1,0:T(8,128)(2,1)} fusion(f32[64,3072]{1,0:T(8,128)} %fusion.4, bf16[1,3072,4096]{2,1,0:T(8,128)(2,1)} %param.11, f32[64,4096]{1,0:T(8,128)S(1)} %fusion.8, bf16[1,3072,4096]{2,1,0:T(8,128)(2,1)} %param.12, f32[64,4096]{1,0:T(8,128)S(1)} %fusion.2, bf16[8,1,8,3072]{3,2,0,1:T(8,128)(2,1)S(1)} %constant_dynamic-update-slice_fusion, ...), kind=kOutput, calls=%fused_computation.19 | convolution fusion | flops 3224436736 | bytes 54001920 | tf_op jit(solution)/shard_map/dot_general | solution.py:50
  95.5 5.2 %all-to-all-start.2 = ((bf16[8,8,3072]{2,1,0:T(8,128)(2,1)}), bf16[8,8,3072]{2,1,0:T(8,128)(2,1)S(1)}, u32[]{:S(2)}, u32[]{:S(2)}) async-start(bf16[8,8,3072]{2,1,0:T(8,128)(2,1)} %fusion.39), calls=%async_computation.2 | async-start | bytes 786432 | tf_op jit(solution)/shard_map/all_to_all | solution.py:115
  100.7 8.7 %all-to-all-done.2 = bf16[8,8,3072]{2,1,0:T(8,128)(2,1)S(1)} async-done(((bf16[8,8,3072]{2,1,0:T(8,128)(2,1)}), bf16[8,8,3072]{2,1,0:T(8,128)(2,1)S(1)}, u32[]{:S(2)}, u32[]{:S(2)}) %all-to-all-start.2) | async-done | bytes 393248 | tf_op jit(solution)/shard_map/all_to_all | solution.py:115
  109.5 1.2 gather_fusion
  110.7 0.0 copy-start.3
  110.7 2.3 %gather_fusion.1 = f32[128,3072]{1,0:T(8,128)} fusion(f32[8,3072]{1,0:T(8,128)S(1)} %get-tuple-element.25, s32[1024]{0:T(1024)S(1)} %pad_clamp_fusion), kind=kCustom, calls=%fused_computation.1 | custom fusion | bytes 3146240 | tf_op jit(solution)/shard_map/gather | solution.py:119
  113.0 1.9 %fusion.52 = bf16[1,128,3072]{2,1,0:T(8,128)(2,1)S(1)} fusion(bf16[1,128,3072]{2,1,0:T(8,128)(2,1)S(1)} %copy-done.3, f32[128,3072]{1,0:T(8,128)} %gather_fusion.1, f32[128,3072]{1,0:T(8,128)S(1)} %gather_fusion, pred[128]{0:T(512)(128)(4,1)S(1)} %get-tuple-element.14, pred[128]{0:T(512)(128)(4,1)S(1)} %get-tuple-element.26), kind=kLoop, calls=%fused_computation.34 | loop fusion | flops 2359296 | bytes 4718848 | tf_op jit(solution)/shard_map/convert_element_type | solution.py:121
  114.9 7.0 %collective-permute-start.7 = (bf16[1,128,3072]{2,1,0:T(8,128)(2,1)S(1)}, bf16[1,128,3072]{2,1,0:T(8,128)(2,1)S(1)}, u32[]{:S(2)}, u32[]{:S(2)}) collective-permute-start(bf16[1,128,3072]{2,1,0:T(8,128)(2,1)S(1)} %fusion.52), channel_id=1, source_target_pairs={{8,0},{16,8},{24,16},{9,1},{17,9},{25,17},{10,2},{18,10},{26,18},{... | collective-permute-start | bytes 2359304 | tf_op jit(solution)/shard_map/ppermute | solution.py:37
  121.9 10.8 %collective-permute-done.7 = bf16[1,128,3072]{2,1,0:T(8,128)(2,1)S(1)} collective-permute-done((bf16[1,128,3072]{2,1,0:T(8,128)(2,1)S(1)}, bf16[1,128,3072]{2,1,0:T(8,128)(2,1)S(1)}, u32[]{:S(2)}, u32[]{:S(2)}) %collective-permute-start.7) | collective-permute-done | bytes 786464 | tf_op jit(solution)/shard_map/ppermute | solution.py:37
  132.7 0.9 copy.26
  (28 shorter events, 0.3 us)
Async XLA Ops:
  0.0 10.9 %copy-start = (bf16[1,128,3072]{2,1,0:T(8,128)(2,1)S(1)}, bf16[1,128,3072]{2,1,0:T(8,128)(2,1)}, u32[]{:S(2)}) copy-start(bf16[1,128,3072]{2,1,0:T(8,128)(2,1)} %param.7) | copy-start | bytes 2359300
  1.0 11.9 %copy-start.4 = (f32[1,128,2]{1,2,0:T(2,128)S(1)}, f32[1,128,2]{1,2,0:T(2,128)}, u32[]{:S(2)}) copy-start(f32[1,128,2]{1,2,0:T(2,128)} %param.10) | copy-start | bytes 3076
  3.9 11.6 %all-to-all-start.1 = ((s32[8,1,1]{2,1,0:T(1,128)}), s32[8,1,1]{2,1,0:T(1,128)S(1)}, u32[]{:S(2)}, u32[]{:S(2)}) async-start(s32[8,1,1]{2,1,0:T(1,128)} %all_to_all.16), calls=%async_computation.1 | async-start | bytes 8192 | tf_op jit(solution)/shard_map/all_to_all | solution.py:102
  10.3 2.9 %copy-start.2 = (bf16[1,128,3072]{2,1,0:T(8,128)(2,1)S(1)}, bf16[1,128,3072]{2,1,0:T(8,128)(2,1)}, u32[]{:S(2)}) copy-start(bf16[1,128,3072]{2,1,0:T(8,128)(2,1)} %param.8) | copy-start | bytes 2359300
  11.4 8.6 %collective-permute-start = (bf16[1,1,8,3072]{3,2,0,1:T(8,128)(2,1)S(1)}, bf16[1,1,8,3072]{3,2,0,1:T(8,128)(2,1)S(1)}, u32[]{:S(2)}, u32[]{:S(2)}) collective-permute-start(bf16[1,1,8,3072]{3,2,0,1:T(8,128)(2,1)S(1)} %constant_dynamic-slice_fusion.6), channel_id=1, source_target_pairs={{0,1},{1,2},{2,3},{3,4},{4,5},{5,6},{6,7},{7,0},{8,9},{9,10},{10,1... | collective-permute-start | bytes 147464 | tf_op jit(solution)/shard_map/ppermute | solution.py:29
  16.3 32.5 %all-to-all-start = ((bf16[8,8,3072]{2,1,0:T(8,128)(2,1)}), bf16[8,8,3072]{2,1,0:T(8,128)(2,1)S(1)}, u32[]{:S(2)}, u32[]{:S(2)}) async-start(bf16[8,8,3072]{2,1,0:T(8,128)(2,1)} %bitcast.5), calls=%async_computation | async-start | bytes 786432 | tf_op jit(solution)/shard_map/all_to_all | solution.py:101
  20.1 9.9 %collective-permute-start.1 = (bf16[1,1,8,3072]{3,2,0,1:T(8,128)(2,1)S(1)}, bf16[1,1,8,3072]{3,2,0,1:T(8,128)(2,1)S(1)}, u32[]{:S(2)}, u32[]{:S(2)}) collective-permute-start(bf16[1,1,8,3072]{3,2,0,1:T(8,128)(2,1)S(1)} %get-tuple-element.22), channel_id=1, source_target_pairs={{0,2},{1,3},{2,4},{3,5},{4,6},{5,7},{6,0},{7,1},{8,10},{9,11},{10,... | collective-permute-start | bytes 147464 | tf_op jit(solution)/shard_map/ppermute | solution.py:29
  22.5 15.7 %collective-permute-start.6 = (bf16[1,1,8,3072]{3,2,0,1:T(8,128)(2,1)S(1)}, bf16[1,1,8,3072]{3,2,0,1:T(8,128)(2,1)S(1)}, u32[]{:S(2)}, u32[]{:S(2)}) collective-permute-start(bf16[1,1,8,3072]{3,2,0,1:T(8,128)(2,1)S(1)} %get-tuple-element.17), channel_id=1, source_target_pairs={{0,7},{1,0},{2,1},{3,2},{4,3},{5,4},{6,5},{7,6},{8,15},{9,8},{10,9... | collective-permute-start | bytes 147464 | tf_op jit(solution)/shard_map/ppermute | solution.py:29
  24.6 13.6 %collective-permute-start.5 = (bf16[1,1,8,3072]{3,2,0,1:T(8,128)(2,1)S(1)}, bf16[1,1,8,3072]{3,2,0,1:T(8,128)(2,1)S(1)}, u32[]{:S(2)}, u32[]{:S(2)}) collective-permute-start(bf16[1,1,8,3072]{3,2,0,1:T(8,128)(2,1)S(1)} %get-tuple-element.18), channel_id=1, source_target_pairs={{0,6},{1,7},{2,0},{3,1},{4,2},{5,3},{6,4},{7,5},{8,14},{9,15},{10,... | collective-permute-start | bytes 147464 | tf_op jit(solution)/shard_map/ppermute | solution.py:29
  25.8 12.4 %collective-permute-start.4 = (bf16[1,1,8,3072]{3,2,0,1:T(8,128)(2,1)S(1)}, bf16[1,1,8,3072]{3,2,0,1:T(8,128)(2,1)S(1)}, u32[]{:S(2)}, u32[]{:S(2)}) collective-permute-start(bf16[1,1,8,3072]{3,2,0,1:T(8,128)(2,1)S(1)} %get-tuple-element.19), channel_id=1, source_target_pairs={{0,5},{1,6},{2,7},{3,0},{4,1},{5,2},{6,3},{7,4},{8,13},{9,14},{10,... | collective-permute-start | bytes 147464 | tf_op jit(solution)/shard_map/ppermute | solution.py:29
  26.1 12.1 %collective-permute-start.3 = (bf16[1,1,8,3072]{3,2,0,1:T(8,128)(2,1)S(1)}, bf16[1,1,8,3072]{3,2,0,1:T(8,128)(2,1)S(1)}, u32[]{:S(2)}, u32[]{:S(2)}) collective-permute-start(bf16[1,1,8,3072]{3,2,0,1:T(8,128)(2,1)S(1)} %get-tuple-element.20), channel_id=1, source_target_pairs={{0,4},{1,5},{2,6},{3,7},{4,0},{5,1},{6,2},{7,3},{8,12},{9,13},{10,... | collective-permute-start | bytes 147464 | tf_op jit(solution)/shard_map/ppermute | solution.py:29
  30.0 8.2 %collective-permute-start.2 = (bf16[1,1,8,3072]{3,2,0,1:T(8,128)(2,1)S(1)}, bf16[1,1,8,3072]{3,2,0,1:T(8,128)(2,1)S(1)}, u32[]{:S(2)}, u32[]{:S(2)}) collective-permute-start(bf16[1,1,8,3072]{3,2,0,1:T(8,128)(2,1)S(1)} %get-tuple-element.21), channel_id=1, source_target_pairs={{0,3},{1,4},{2,5},{3,6},{4,7},{5,0},{6,1},{7,2},{8,11},{9,12},{10,... | collective-permute-start | bytes 147464 | tf_op jit(solution)/shard_map/ppermute | solution.py:29
  95.5 13.9 %all-to-all-start.2 = ((bf16[8,8,3072]{2,1,0:T(8,128)(2,1)}), bf16[8,8,3072]{2,1,0:T(8,128)(2,1)S(1)}, u32[]{:S(2)}, u32[]{:S(2)}) async-start(bf16[8,8,3072]{2,1,0:T(8,128)(2,1)} %fusion.39), calls=%async_computation.2 | async-start | bytes 786432 | tf_op jit(solution)/shard_map/all_to_all | solution.py:115
  110.7 2.3 %copy-start.3 = (bf16[1,128,3072]{2,1,0:T(8,128)(2,1)S(1)}, bf16[1,128,3072]{2,1,0:T(8,128)(2,1)}, u32[]{:S(2)}) copy-start(bf16[1,128,3072]{2,1,0:T(8,128)(2,1)} %param.8) | copy-start | bytes 2359300
  113.0 20.6 %copy-start.1 = (bf16[1,128,3072]{2,1,0:T(8,128)(2,1)S(1)}, bf16[1,128,3072]{2,1,0:T(8,128)(2,1)}, u32[]{:S(2)}) copy-start(bf16[1,128,3072]{2,1,0:T(8,128)(2,1)} %param.7) | copy-start | bytes 2359300
  114.9 17.8 %collective-permute-start.7 = (bf16[1,128,3072]{2,1,0:T(8,128)(2,1)S(1)}, bf16[1,128,3072]{2,1,0:T(8,128)(2,1)S(1)}, u32[]{:S(2)}, u32[]{:S(2)}) collective-permute-start(bf16[1,128,3072]{2,1,0:T(8,128)(2,1)S(1)} %fusion.52), channel_id=1, source_target_pairs={{8,0},{16,8},{24,16},{9,1},{17,9},{25,17},{10,2},{18,10},{26,18},{... | collective-permute-start | bytes 2359304 | tf_op jit(solution)/shard_map/ppermute | solution.py:37
